TPU v7x, 256 devices: a whole 4x4x8 slice. The times are simulated.
256 devices in a mesh: seq: 64 (over z, y, core), ch: 4 (over x).
Axes of the slice: x: 4, y: 4, z: 8, core: 2. Of those that a mesh axis runs over, the one named last changes fastest.
Arguments:
- query_proj: bfloat16 [8192, 2048], P('seq', 'ch'), may hold values from -6 to 6
- key_proj: bfloat16 [8192, 2048], P('seq', 'ch'), may hold values from -6 to 6
- value_proj: bfloat16 [8192, 2048], P('seq', 'ch'), may hold values from -6 to 6
- short_filter: float32 [3, 3, 2048], P(None, None, 'ch'), may hold values from -3.5 to 3.5
- long_filter: float32 [8192, 2048], P('seq', 'ch'), may hold values from -0.0625 to 0.0625
- skip_gain: float32 [2048], P('ch'), may hold values from 0.5 to 1.5
- out_weight: bfloat16 [2048, 4096], P('ch'), may hold values from -0.125 to 0.125
- cotangent: bfloat16 [8192, 4096], P('seq', 'ch'), may hold values from -16 to 16
Outputs:
- layer_out: bfloat16 [8192, 4096], P('seq', 'ch')
- grad_query: float32 [8192, 2048], P('seq', 'ch')
- grad_key: float32 [8192, 2048], P('seq', 'ch')
- grad_value: float32 [8192, 2048], P('seq', 'ch')
- grad_short: float32 [3, 3, 2048], P(None, None, 'ch')
- grad_filter: float32 [8192, 2048], P('seq', 'ch')
- grad_skip: float32 [2048], P('ch')
- grad_w_out_t: float32 [4096, 2048], P('seq', 'ch')
All inputs are finite; a program needn't handle non-finite values.
Results may differ from a plain program's by a relative error of at most 0.011.
Values may be sent and summed in bfloat16 or wider, within the bound.
A program may use at most 128 MiB of HBM per device.

v0:
```python
import math
import jax
import jax.numpy as jnp
from jax import lax
from jax.sharding import PartitionSpec as P

exact_mode = lax.Precision.HIGHEST


def from_behind(shard, axis, by):
    size = lax.axis_size(axis)
    pairs = [(i, i + by) for i in range(size) if 0 <= i + by < size]
    return lax.ppermute(shard, axis, pairs)


def as_sent(shard):

    def short(part):
        return part.astype(jnp.bfloat16) if part.dtype == jnp.float32 else part

    return jax.tree.map(short, shard)


def tables(rows_out, cols_in, period):
    row_index = lax.broadcasted_iota(jnp.int32, (rows_out, cols_in), 0)
    col_index = lax.broadcasted_iota(jnp.int32, (rows_out, cols_in), 1)
    phase_angle = (row_index * col_index % period).astype(jnp.float32) * (2.0 * math.pi / period)
    return (jnp.cos(phase_angle), jnp.sin(phase_angle))


def along_rows(factor, values):
    return jnp.tensordot(factor, values, axes=1, precision=exact_mode)


def rows_spectrum(signal, basis_pair):
    return (along_rows(basis_pair[0], signal), -along_rows(basis_pair[1], signal))


def rows_inverse(complex_pair, basis_pair):
    total = along_rows(basis_pair[0], complex_pair[0]) - along_rows(basis_pair[1], complex_pair[1])
    return total / basis_pair[0].shape[1]


def block_forward(complex_pair, basis_pair):
    cosine_part, sine_part = basis_pair
    real_part = along_rows(cosine_part, complex_pair[0]) + along_rows(sine_part, complex_pair[1])
    imag_part = along_rows(cosine_part, complex_pair[1]) - along_rows(sine_part, complex_pair[0])
    return (real_part, imag_part)


def block_inverse(complex_pair, basis_pair):
    cosine_part, sine_part = basis_pair
    norming = 1.0 / cosine_part.shape[1]
    real_part = along_rows(cosine_part, complex_pair[0]) - along_rows(sine_part, complex_pair[1])
    imag_part = along_rows(cosine_part, complex_pair[1]) + along_rows(sine_part, complex_pair[0])
    return (real_part * norming, imag_part * norming)


def complex_product(first_pair, second_pair):
    return (
        first_pair[0] * second_pair[0] - first_pair[1] * second_pair[1],
        first_pair[0] * second_pair[1] + first_pair[1] * second_pair[0],
    )


def conj_product(first_pair, second_pair):
    return (
        first_pair[0] * second_pair[0] + first_pair[1] * second_pair[1],
        first_pair[0] * second_pair[1] - first_pair[1] * second_pair[0],
    )


def on_device(
    query_proj, key_proj, value_proj, short_filter, long_filter, skip_gain, out_weight, cotangent
):
    block_rows = query_proj.shape[0]
    tap_count = short_filter.shape[1]
    block_count = lax.axis_size("seq")
    streams = jnp.stack([query_proj, key_proj, value_proj])
    earlier = from_behind(streams[:, block_rows - (tap_count - 1) :], "seq", 1)
    extended = jnp.concatenate([earlier, streams], axis=1).astype(jnp.float32)
    shifted = [
        extended[:, tap_count - 1 - offset : tap_count - 1 - offset + block_rows]
        for offset in range(tap_count)
    ]
    filtered = sum(
        (short_filter[:, offset][:, None, :] * shifted[offset] for offset in range(tap_count))
    )
    query_short, key_short, value_short = (filtered[0], filtered[1], filtered[2])
    product = key_short * value_short
    forward_basis = tables(2 * block_rows, block_rows, 2 * block_rows)
    full_basis = tables(2 * block_rows, 2 * block_rows, 2 * block_rows)
    half_basis = tables(block_rows, 2 * block_rows, 2 * block_rows)
    block_basis = tables(2 * block_count, block_count, 2 * block_count)
    return_basis = tables(block_count, 2 * block_count, 2 * block_count)
    input_pair = rows_spectrum(product, forward_basis)
    filter_pair = rows_spectrum(long_filter, forward_basis)
    moved_data = (
        lax.all_to_all(input_pair[0][None], "seq", split_axis=1, concat_axis=0, tiled=True),
        lax.all_to_all(input_pair[1][None], "seq", split_axis=1, concat_axis=0, tiled=True),
        lax.all_to_all(filter_pair[0][None], "seq", split_axis=1, concat_axis=0, tiled=True),
        lax.all_to_all(filter_pair[1][None], "seq", split_axis=1, concat_axis=0, tiled=True),
    )
    input_spectrum = block_forward((moved_data[0], moved_data[1]), block_basis)
    filter_spectrum = block_forward((moved_data[2], moved_data[3]), block_basis)
    inverse_pair = block_inverse(complex_product(filter_spectrum, input_spectrum), return_basis)
    returned = (
        lax.all_to_all(inverse_pair[0], "seq", split_axis=0, concat_axis=1, tiled=True),
        lax.all_to_all(inverse_pair[1], "seq", split_axis=0, concat_axis=1, tiled=True),
    )
    folded = rows_inverse((returned[0][0], returned[1][0]), full_basis)
    carried = from_behind(folded[block_rows:], "seq", 1)
    convolved = folded[:block_rows] + carried
    mixed_seq = convolved + skip_gain * product
    gated_values = (query_short * mixed_seq).astype(jnp.bfloat16)
    partial_value = jnp.dot(gated_values, out_weight, preferred_element_type=jnp.float32)
    layer_out = lax.psum_scatter(partial_value, "ch", scatter_dimension=1, tiled=True).astype(
        jnp.bfloat16
    )
    full_cotangent = lax.all_gather(cotangent, "ch", axis=1, tiled=True)
    grad_gated = lax.dot_general(
        full_cotangent, out_weight, (((1,), (1,)), ((), ())), preferred_element_type=jnp.float32
    )
    grad_w_out_t = lax.psum_scatter(
        lax.dot_general(
            full_cotangent,
            gated_values,
            (((0,), (0,)), ((), ())),
            preferred_element_type=jnp.float32,
        ),
        "seq",
        scatter_dimension=0,
        tiled=True,
    )
    grad_mixed = grad_gated * query_short
    grad_query_short = grad_gated * mixed_seq
    following = from_behind(grad_mixed.astype(jnp.bfloat16), "seq", -1).astype(grad_mixed.dtype)
    spread = jnp.concatenate([grad_mixed, following], axis=0)
    grad_pair = rows_spectrum(spread, full_basis)
    moved_grad = (
        lax.all_to_all(
            grad_pair[0][None].astype(jnp.bfloat16), "seq", split_axis=1, concat_axis=0, tiled=True
        ).astype(jnp.float32),
        lax.all_to_all(
            grad_pair[1][None].astype(jnp.bfloat16), "seq", split_axis=1, concat_axis=0, tiled=True
        ).astype(jnp.float32),
    )
    grad_spectrum = block_forward(moved_grad, block_basis)
    input_back = block_inverse(conj_product(filter_spectrum, grad_spectrum), return_basis)
    filter_back = block_inverse(conj_product(input_spectrum, grad_spectrum), return_basis)
    returned_grad = (
        lax.all_to_all(as_sent(input_back[0]), "seq", split_axis=0, concat_axis=1, tiled=True),
        lax.all_to_all(as_sent(input_back[1]), "seq", split_axis=0, concat_axis=1, tiled=True),
        lax.all_to_all(as_sent(filter_back[0]), "seq", split_axis=0, concat_axis=1, tiled=True),
        lax.all_to_all(as_sent(filter_back[1]), "seq", split_axis=0, concat_axis=1, tiled=True),
    )
    conv_grad = rows_inverse((returned_grad[0][0], returned_grad[1][0]), half_basis)
    grad_filter = rows_inverse((returned_grad[2][0], returned_grad[3][0]), half_basis)
    grad_product = conv_grad + skip_gain * grad_mixed
    grad_streams = jnp.stack(
        [grad_query_short, grad_product * value_short, grad_product * key_short]
    )
    later_rows = from_behind(grad_streams[:, : tap_count - 1], "seq", -1)
    padded_grad = jnp.concatenate([grad_streams, later_rows], axis=1)
    grad_inputs = sum(
        (
            short_filter[:, offset][:, None, :] * padded_grad[:, offset : offset + block_rows]
            for offset in range(tap_count)
        )
    )
    short_terms = jnp.stack(
        [jnp.sum(grad_streams * shifted[offset], axis=1) for offset in range(tap_count)], axis=1
    )
    skip_terms = jnp.sum(grad_mixed * product, axis=0)
    grad_short, grad_skip = lax.psum((short_terms, skip_terms), "seq")
    return (
        layer_out,
        grad_inputs[0],
        grad_inputs[1],
        grad_inputs[2],
        grad_short,
        grad_filter,
        grad_skip,
        grad_w_out_t,
    )


def solution(mesh):
    in_specs = (
        P("seq", "ch"),
        P("seq", "ch"),
        P("seq", "ch"),
        P(None, None, "ch"),
        P("seq", "ch"),
        P("ch"),
        P("ch", None),
        P("seq", "ch"),
    )
    out_specs = (
        P("seq", "ch"),
        P("seq", "ch"),
        P("seq", "ch"),
        P("seq", "ch"),
        P(None, None, "ch"),
        P("seq", "ch"),
        P("ch"),
        P("seq", "ch"),
    )
    return jax.shard_map(
        on_device, mesh=mesh, in_specs=in_specs, out_specs=out_specs, check_vma=False
    )
```

profile of v0, /device:TPU:128, one launch (start us, length us, event | category | flops | bytes accessed | tf_op | source)
XLA Modules:
  0.0 595.5 jit_solution(4163369998278943151)
XLA Ops:
  10.5 10.5 %all-to-all-start.1 = ((f32[1,256,512]{2,0,1:T(1,128)}), f32[1,256,512]{2,0,1:T(1,128)S(1)}, u32[]{:S(2)}, u32[]{:S(2)}) async-start(f32[1,256,512]{2,0,1:T(1,128)} %copy.65), calls=%async_computation.1 | async-start | bytes 1048576 | tf_op jit(solution)/shard_map/all_to_all | solution.py:102
  27.0 8.9 %all-to-all-done.1 = f32[1,256,512]{2,0,1:T(1,128)S(1)} async-done(((f32[1,256,512]{2,0,1:T(1,128)}), f32[1,256,512]{2,0,1:T(1,128)S(1)}, u32[]{:S(2)}, u32[]{:S(2)}) %all-to-all-start.1) | async-done | bytes 524320 | tf_op jit(solution)/shard_map/all_to_all | solution.py:102
  35.9 8.6 %all-to-all-start = ((f32[1,256,512]{2,0,1:T(1,128)}), f32[1,256,512]{2,0,1:T(1,128)S(1)}, u32[]{:S(2)}, u32[]{:S(2)}) async-start(f32[1,256,512]{2,0,1:T(1,128)} %copy.63), calls=%async_computation | async-start | bytes 1048576 | tf_op jit(solution)/shard_map/all_to_all | solution.py:101
  44.9 6.6 %all-gather.2.cloned.1.call-done = bf16[128,4096]{1,0:T(8,128)(2,1)} async-done(((bf16[128,1024]{1,0:T(8,128)(2,1)}), bf16[128,4096]{1,0:T(8,128)(2,1)}) %all-gather.2.cloned.1.call-update) | async-done | bytes 1048592 | tf_op jit(solution)/shard_map/all_gather | solution.py:120
  51.5 4.8 multiply_reduce_fusion.3
  56.3 3.1 collective-permute-start.2
  59.4 2.5 collective-permute-done.2
  68.3 12.3 %all-to-all-start.6 = ((bf16[64,2,1024]{2,1,0:T(2,128)(2,1)}), bf16[64,2,1024]{2,1,0:T(2,128)(2,1)}, u32[]{:S(2)}, u32[]{:S(2)}) async-start(bf16[64,2,1024]{2,1,0:T(2,128)(2,1)} %reshape.75), calls=%async_computation.7 | async-start | bytes 524288 | tf_op jit(solution)/shard_map/all_to_all | solution.py:141
  82.0 2.6 fusion.15
  89.6 9.1 %all-to-all-start.7 = ((bf16[64,2,1024]{2,1,0:T(2,128)(2,1)}), bf16[64,2,1024]{2,1,0:T(2,128)(2,1)}, u32[]{:S(2)}, u32[]{:S(2)}) async-start(bf16[64,2,1024]{2,1,0:T(2,128)(2,1)} %reshape.73), calls=%async_computation.8 | async-start | bytes 524288 | tf_op jit(solution)/shard_map/all_to_all | solution.py:144
  107.9 10.4 %all-to-all-start.3 = ((f32[1,256,512]{2,0,1:T(1,128)}), f32[1,256,512]{2,0,1:T(1,128)S(1)}, u32[]{:S(2)}, u32[]{:S(2)}) async-start(f32[1,256,512]{2,0,1:T(1,128)} %copy.69), calls=%async_computation.3 | async-start | bytes 1048576 | tf_op jit(solution)/shard_map/all_to_all | solution.py:100
  133.2 8.8 %all-to-all-start.2 = ((f32[1,256,512]{2,0,1:T(1,128)}), f32[1,256,512]{2,0,1:T(1,128)S(1)}, u32[]{:S(2)}, u32[]{:S(2)}) async-start(f32[1,256,512]{2,0,1:T(1,128)} %copy.67), calls=%async_computation.2 | async-start | bytes 1048576 | tf_op jit(solution)/shard_map/all_to_all | solution.py:99
  148.4 8.3 %all-to-all-done.2 = f32[1,256,512]{2,0,1:T(1,128)S(1)} async-done(((f32[1,256,512]{2,0,1:T(1,128)}), f32[1,256,512]{2,0,1:T(1,128)S(1)}, u32[]{:S(2)}, u32[]{:S(2)}) %all-to-all-start.2) | async-done | bytes 524320 | tf_op jit(solution)/shard_map/all_to_all | solution.py:99
  161.6 5.8 multiply_subtract_fusion
  171.4 8.7 %all-to-all-start.8 = ((bf16[64,4,512]{2,1,0:T(4,128)(2,1)}), bf16[64,4,512]{2,1,0:T(4,128)(2,1)}, u32[]{:S(2)}, u32[]{:S(2)}) async-start(bf16[64,4,512]{2,1,0:T(4,128)(2,1)} %copy.83), calls=%async_computation.9 | async-start | bytes 524288 | tf_op jit(solution)/shard_map/all_to_all | solution.py:152
  185.3 4.0 all-to-all-done.8
  189.3 9.1 %all-to-all-start.4 = ((f32[64,4,512]{2,1,0:T(4,128)}), f32[64,4,512]{2,1,0:T(4,128)}, u32[]{:S(2)}, u32[]{:S(2)}) async-start(f32[64,4,512]{2,1,0:T(4,128)} %copy.75), calls=%async_computation.4 | async-start | bytes 1048576 | tf_op jit(solution)/shard_map/all_to_all | solution.py:108
  203.6 9.7 %all-to-all-done.4 = f32[64,4,512]{2,1,0:T(4,128)} async-done(((f32[64,4,512]{2,1,0:T(4,128)}), f32[64,4,512]{2,1,0:T(4,128)}, u32[]{:S(2)}, u32[]{:S(2)}) %all-to-all-start.4) | async-done | bytes 524320 | tf_op jit(solution)/shard_map/all_to_all | solution.py:108
  213.3 8.7 %all-to-all-start.5 = ((f32[64,4,512]{2,1,0:T(4,128)}), f32[64,4,512]{2,1,0:T(4,128)}, u32[]{:S(2)}, u32[]{:S(2)}) async-start(f32[64,4,512]{2,1,0:T(4,128)} %copy.76), calls=%async_computation.5 | async-start | bytes 1048576 | tf_op jit(solution)/shard_map/all_to_all | solution.py:109
  229.5 7.3 %all-to-all-done.5 = f32[64,4,512]{2,1,0:T(4,128)} async-done(((f32[64,4,512]{2,1,0:T(4,128)}), f32[64,4,512]{2,1,0:T(4,128)}, u32[]{:S(2)}, u32[]{:S(2)}) %all-to-all-start.5) | async-done | bytes 524320 | tf_op jit(solution)/shard_map/all_to_all | solution.py:109
  236.8 8.7 %all-to-all-start.9 = ((bf16[64,4,512]{2,1,0:T(4,128)(2,1)}), bf16[64,4,512]{2,1,0:T(4,128)(2,1)}, u32[]{:S(2)}, u32[]{:S(2)}) async-start(bf16[64,4,512]{2,1,0:T(4,128)(2,1)} %copy.84), calls=%async_computation.10 | async-start | bytes 524288 | tf_op jit(solution)/shard_map/all_to_all | solution.py:153
  245.7 3.5 fusion.61
  251.3 2.8 fusion.8
  263.8 3.2 collective-permute-done.1
  271.7 5.4 convolution_bitcast_fusion
  277.1 9.1 %copy.89 = f32[4096,512]{1,0:T(8,128)} copy(f32[4096,512]{0,1:T(8,128)} %convolution_bitcast_fusion) | data formatting | bytes 16777216
  289.1 8.5 %all-to-all-start.11 = ((bf16[64,4,512]{2,1,0:T(4,128)(2,1)}), bf16[64,4,512]{2,1,0:T(4,128)(2,1)}, u32[]{:S(2)}, u32[]{:S(2)}) async-start(bf16[64,4,512]{2,1,0:T(4,128)(2,1)} %copy.86), calls=%async_computation.12 | async-start | bytes 524288 | tf_op jit(solution)/shard_map/all_to_all | solution.py:155
  300.2 6.4 %all-to-all-done.11 = bf16[64,4,512]{2,1,0:T(4,128)(2,1)} async-done(((bf16[64,4,512]{2,1,0:T(4,128)(2,1)}), bf16[64,4,512]{2,1,0:T(4,128)(2,1)}, u32[]{:S(2)}, u32[]{:S(2)}) %all-to-all-start.11) | async-done | bytes 262176 | tf_op jit(solution)/shard_map/all_to_all | solution.py:155
  306.6 8.6 %all-to-all-start.10 = ((bf16[64,4,512]{2,1,0:T(4,128)(2,1)}), bf16[64,4,512]{2,1,0:T(4,128)(2,1)S(1)}, u32[]{:S(2)}, u32[]{:S(2)}) async-start(bf16[64,4,512]{2,1,0:T(4,128)(2,1)} %copy.85), calls=%async_computation.11 | async-start | bytes 524288 | tf_op jit(solution)/shard_map/all_to_all | solution.py:154
  316.3 8.2 %all-to-all-done.10 = bf16[64,4,512]{2,1,0:T(4,128)(2,1)S(1)} async-done(((bf16[64,4,512]{2,1,0:T(4,128)(2,1)}), bf16[64,4,512]{2,1,0:T(4,128)(2,1)S(1)}, u32[]{:S(2)}, u32[]{:S(2)}) %all-to-all-start.10) | async-done | bytes 262176 | tf_op jit(solution)/shard_map/all_to_all | solution.py:154
  325.4 4.2 collective-permute-start.3
  333.7 251.7 %all-reduce = (f32[3,3,512]{2,0,1:T(4,128)S(1)}, f32[512]{0:T(512)}) all-reduce(f32[3,3,512]{2,0,1:T(4,128)S(1)} %pad_maximum_fusion.5, f32[512]{0:T(512)S(1)} %get-tuple-element.45), channel_id=1, replica_groups=mesh['seq'=64,'ch'=4] {'seq'}, use_global_device_ids=true, to_apply=%region_4.5 | all-reduce | flops 5120 | bytes 40960 | tf_op jit(solution)/shard_map/psum | solution.py:175
  (150 shorter events, 110.5 us)
Async XLA Ops:
  7.2 37.3 %copy-start.16 = (bf16[128,512]{1,0:T(8,128)(2,1)S(1)}, bf16[128,512]{1,0:T(8,128)(2,1)}, u32[]{:S(2)}) copy-start(bf16[128,512]{1,0:T(8,128)(2,1)} %param.10) | copy-start | bytes 393220
  7.2 37.3 %copy-start.17 = (bf16[128,512]{1,0:T(8,128)(2,1)S(1)}, bf16[128,512]{1,0:T(8,128)(2,1)}, u32[]{:S(2)}) copy-start(bf16[128,512]{1,0:T(8,128)(2,1)} %param.9) | copy-start | bytes 393220
  7.2 37.3 %copy-start.18 = (bf16[128,512]{1,0:T(8,128)(2,1)S(1)}, bf16[128,512]{1,0:T(8,128)(2,1)}, u32[]{:S(2)}) copy-start(bf16[128,512]{1,0:T(8,128)(2,1)} %param.8) | copy-start | bytes 393220
  7.2 19.8 %copy-start.20 = (f32[3,3,512]{2,1,0:T(4,128)S(1)}, f32[3,3,512]{2,1,0:T(4,128)}, u32[]{:S(2)}) copy-start(f32[3,3,512]{2,1,0:T(4,128)} %param.11) | copy-start | bytes 55300
  10.5 25.4 %all-to-all-start.1 = ((f32[1,256,512]{2,0,1:T(1,128)}), f32[1,256,512]{2,0,1:T(1,128)S(1)}, u32[]{:S(2)}, u32[]{:S(2)}) async-start(f32[1,256,512]{2,0,1:T(1,128)} %copy.65), calls=%async_computation.1 | async-start | bytes 1048576 | tf_op jit(solution)/shard_map/all_to_all | solution.py:102
  21.0 30.5 %all-gather.2.cloned.1.call-start = ((), (), s32[]{:S(2)}) async-start(), calls=%async_computation.15 | async-start | bytes 1310720 | tf_op jit(solution)/shard_map/all_gather | solution.py:120
  22.5 22.0 %collective-permute-start = (bf16[3,2,512]{2,1,0:T(2,128)(2,1)S(1)}, bf16[3,2,512]{2,1,0:T(2,128)(2,1)S(1)}, u32[]{:S(2)}, u32[]{:S(2)}) collective-permute-start(bf16[3,2,512]{2,1,0:T(2,128)(2,1)S(1)} %pad_maximum_fusion.6), channel_id=1, source_target_pairs={{0,4},{4,8},{8,12},{12,16},{16,20},{20,24},{24,28},{28,32},{32,36}... | collective-permute-start | bytes 18440 | tf_op jit(solution)/shard_map/ppermute | solution.py:13
  35.9 8.6 %copy-start.12 = (f32[1,256,512]{2,0,1:T(1,128)}, f32[1,256,512]{2,0,1:T(1,128)S(1)}, u32[]{:S(2)}) copy-start(f32[1,256,512]{2,0,1:T(1,128)S(1)} %all-to-all-done.1) | copy-start | bytes 1572868
  35.9 32.4 %all-to-all-start = ((f32[1,256,512]{2,0,1:T(1,128)}), f32[1,256,512]{2,0,1:T(1,128)S(1)}, u32[]{:S(2)}, u32[]{:S(2)}) async-start(f32[1,256,512]{2,0,1:T(1,128)} %copy.63), calls=%async_computation | async-start | bytes 1048576 | tf_op jit(solution)/shard_map/all_to_all | solution.py:101
  44.9 19.3 %copy-start.6 = (f32[3,128,512]{2,1,0:T(8,128)}, f32[3,128,512]{2,1,0:T(8,128)S(1)}, u32[]{:S(2)}) copy-start(f32[3,128,512]{2,1,0:T(8,128)S(1)} %multiply_add_fusion.3) | copy-start | bytes 2359300
  56.3 5.6 collective-permute-start.2
  68.3 31.6 %copy-start.13 = (f32[1,256,512]{2,0,1:T(1,128)S(1)}, f32[1,256,512]{2,0,1:T(1,128)}, u32[]{:S(2)}) copy-start(f32[1,256,512]{2,0,1:T(1,128)} %copy-done.12) | copy-start | bytes 1572868
  68.3 21.3 %all-to-all-start.6 = ((bf16[64,2,1024]{2,1,0:T(2,128)(2,1)}), bf16[64,2,1024]{2,1,0:T(2,128)(2,1)}, u32[]{:S(2)}, u32[]{:S(2)}) async-start(bf16[64,2,1024]{2,1,0:T(2,128)(2,1)} %reshape.75), calls=%async_computation.7 | async-start | bytes 524288 | tf_op jit(solution)/shard_map/all_to_all | solution.py:141
  89.6 18.3 %all-to-all-start.7 = ((bf16[64,2,1024]{2,1,0:T(2,128)(2,1)}), bf16[64,2,1024]{2,1,0:T(2,128)(2,1)}, u32[]{:S(2)}, u32[]{:S(2)}) async-start(bf16[64,2,1024]{2,1,0:T(2,128)(2,1)} %reshape.73), calls=%async_computation.8 | async-start | bytes 524288 | tf_op jit(solution)/shard_map/all_to_all | solution.py:144
  107.9 25.3 %all-to-all-start.3 = ((f32[1,256,512]{2,0,1:T(1,128)}), f32[1,256,512]{2,0,1:T(1,128)S(1)}, u32[]{:S(2)}, u32[]{:S(2)}) async-start(f32[1,256,512]{2,0,1:T(1,128)} %copy.69), calls=%async_computation.3 | async-start | bytes 1048576 | tf_op jit(solution)/shard_map/all_to_all | solution.py:100
  133.2 23.5 %all-to-all-start.2 = ((f32[1,256,512]{2,0,1:T(1,128)}), f32[1,256,512]{2,0,1:T(1,128)S(1)}, u32[]{:S(2)}, u32[]{:S(2)}) async-start(f32[1,256,512]{2,0,1:T(1,128)} %copy.67), calls=%async_computation.2 | async-start | bytes 1048576 | tf_op jit(solution)/shard_map/all_to_all | solution.py:99
  171.4 17.9 %all-to-all-start.8 = ((bf16[64,4,512]{2,1,0:T(4,128)(2,1)}), bf16[64,4,512]{2,1,0:T(4,128)(2,1)}, u32[]{:S(2)}, u32[]{:S(2)}) async-start(bf16[64,4,512]{2,1,0:T(4,128)(2,1)} %copy.83), calls=%async_computation.9 | async-start | bytes 524288 | tf_op jit(solution)/shard_map/all_to_all | solution.py:152
  189.3 24.0 %all-to-all-start.4 = ((f32[64,4,512]{2,1,0:T(4,128)}), f32[64,4,512]{2,1,0:T(4,128)}, u32[]{:S(2)}, u32[]{:S(2)}) async-start(f32[64,4,512]{2,1,0:T(4,128)} %copy.75), calls=%async_computation.4 | async-start | bytes 1048576 | tf_op jit(solution)/shard_map/all_to_all | solution.py:108
  213.3 23.5 %all-to-all-start.5 = ((f32[64,4,512]{2,1,0:T(4,128)}), f32[64,4,512]{2,1,0:T(4,128)}, u32[]{:S(2)}, u32[]{:S(2)}) async-start(f32[64,4,512]{2,1,0:T(4,128)} %copy.76), calls=%async_computation.5 | async-start | bytes 1048576 | tf_op jit(solution)/shard_map/all_to_all | solution.py:109
  224.8 37.0 %copy-start.21 = (f32[512]{0:T(512)S(1)}, f32[512]{0:T(512)}, u32[]{:S(2)}) copy-start(f32[512]{0:T(512)} %param.13) | copy-start | bytes 6148
  227.4 39.5 %copy-start.15 = (f32[128,512]{1,0:T(8,128)S(1)}, f32[128,512]{1,0:T(8,128)}, u32[]{:S(2)}) copy-start(f32[128,512]{1,0:T(8,128)} %get-tuple-element.70) | copy-start | bytes 786436
  236.8 23.3 %all-to-all-start.9 = ((bf16[64,4,512]{2,1,0:T(4,128)(2,1)}), bf16[64,4,512]{2,1,0:T(4,128)(2,1)}, u32[]{:S(2)}, u32[]{:S(2)}) async-start(bf16[64,4,512]{2,1,0:T(4,128)(2,1)} %copy.84), calls=%async_computation.10 | async-start | bytes 524288 | tf_op jit(solution)/shard_map/all_to_all | solution.py:153
  245.5 23.3 %copy-start.7 = (f32[3,128,512]{2,1,0:T(8,128)S(1)}, f32[3,128,512]{2,1,0:T(8,128)}, u32[]{:S(2)}) copy-start(f32[3,128,512]{2,1,0:T(8,128)} %copy-done.6) | copy-start | bytes 2359300
  245.5 341.4 %reduce-scatter.5.cloned.1.call-start = ((), (), s32[]{:S(2)}) async-start(), calls=%async_computation.14 | async-start | bytes 2621440 | tf_op jit(solution)/shard_map/reduce_scatter | solution.py:117
  255.6 11.3 %collective-permute-start.1 = (f32[128,512]{1,0:T(8,128)}, f32[128,512]{1,0:T(8,128)}, u32[]{:S(2)}, u32[]{:S(2)}) collective-permute-start(f32[128,512]{1,0:T(8,128)} %slice.82), channel_id=1, source_target_pairs={{0,4},{4,8},{8,12},{12,16},{16,20},{20,24},{24,28},{28,32},{32,36}... | collective-permute-start | bytes 786440 | tf_op jit(solution)/shard_map/ppermute | solution.py:13
  268.9 56.4 %copy-start.9 = (f32[1,128,512]{2,1,0:T(8,128)}, f32[1,128,512]{2,1,0:T(8,128)S(1)}, u32[]{:S(2)}) copy-start(f32[1,128,512]{2,1,0:T(8,128)S(1)} %get-tuple-element.61) | copy-start | bytes 786436
  271.6 317.0 %reduce-scatter.7.cloned.1.call-start = ((), (), s32[]{:S(2)}) async-start(), calls=%async_computation.16 | async-start | bytes 8519680
  289.1 17.5 %all-to-all-start.11 = ((bf16[64,4,512]{2,1,0:T(4,128)(2,1)}), bf16[64,4,512]{2,1,0:T(4,128)(2,1)}, u32[]{:S(2)}, u32[]{:S(2)}) async-start(bf16[64,4,512]{2,1,0:T(4,128)(2,1)} %copy.86), calls=%async_computation.12 | async-start | bytes 524288 | tf_op jit(solution)/shard_map/all_to_all | solution.py:155
  298.5 26.9 %copy-start.10 = (f32[1,128,512]{2,1,0:T(8,128)S(1)}, f32[1,128,512]{2,1,0:T(8,128)}, u32[]{:S(2)}) copy-start(f32[1,128,512]{2,1,0:T(8,128)} %get-tuple-element.48) | copy-start | bytes 786436
  306.6 17.9 %all-to-all-start.10 = ((bf16[64,4,512]{2,1,0:T(4,128)(2,1)}), bf16[64,4,512]{2,1,0:T(4,128)(2,1)S(1)}, u32[]{:S(2)}, u32[]{:S(2)}) async-start(bf16[64,4,512]{2,1,0:T(4,128)(2,1)} %copy.85), calls=%async_computation.11 | async-start | bytes 524288 | tf_op jit(solution)/shard_map/all_to_all | solution.py:154
  325.4 5.7 collective-permute-start.3
  331.1 257.6 %copy-start.1 = (f32[128,512]{1,0:T(8,128)S(1)}, f32[128,512]{1,0:T(8,128)}, u32[]{:S(2)}) copy-start(f32[128,512]{1,0:T(8,128)} %param.12) | copy-start | bytes 786436
  (9 other events, 17.6 us)
Sparse Core Ops, SparseCore 0:
  23.7 27.7 all-gather.1
  271.8 30.2 reduce-scatter.4
  307.4 149.4 reduce-scatter.6
where the time goes:
time: 606 us; the launch traced here: 595 us
  blocking collectives  252 us (42%)
  starting transfers between devices  124 us (20%)
  matrix products  70.6 us (12%)
  waiting for transfers between devices  69 us (11%)
  local copies, waits for them, and re-layouts  47.8 us (8%)
  other arithmetic  17.7 us (3%)
  between operations  14.7 us (2%)
    psum x1, blocking collectives, on_device(): grad_short, grad_skip = lax.psum((short_terms, skip_terms), 'seq')  252 us
    dot_general x36, matrix products, along_rows(): return jnp.tensordot(factor, values, axes=1, precision=exact_mode)  58.4 us
    unnamed x53, local copies, waits for them, and re-layouts  20.7 us
    all_to_all x1, starting transfers between devices, on_device(): lax.all_to_all(grad_pair[0][None].astype(jnp.bfloat16), 'seq', split_axis...  12.3 us
  transfers between devices with their start and end apart: 19, of which 13 were waited for; matrix products, arithmetic and copies ran while one was open for 18% of the time, Pallas kernels for 0%

commit v1 on v0

--- a/solution.py
+++ b/solution.py
@@ -3,6 +3,7 @@
 import jax.numpy as jnp
 from jax import lax
 from jax.sharding import PartitionSpec as P
+from jax.lax import all_to_all, axis_size
 
 exact_mode = lax.Precision.HIGHEST
 
@@ -73,6 +74,14 @@
 def on_device(
     query_proj, key_proj, value_proj, short_filter, long_filter, skip_gain, out_weight, cotangent
 ):
+
+    def do_stocks(s0):
+        piece_now = axis_size("seq")
+        later = jnp.split(s0, piece_now, axis=1)
+        carry_out = jnp.stack(later)
+        y = all_to_all(carry_out, axis_name="seq", split_axis=0, concat_axis=0)
+        return jnp.concatenate(y, axis=0)
+
     block_rows = query_proj.shape[0]
     tap_count = short_filter.shape[1]
     block_count = lax.axis_size("seq")
@@ -99,7 +108,7 @@
         lax.all_to_all(input_pair[0][None], "seq", split_axis=1, concat_axis=0, tiled=True),
         lax.all_to_all(input_pair[1][None], "seq", split_axis=1, concat_axis=0, tiled=True),
         lax.all_to_all(filter_pair[0][None], "seq", split_axis=1, concat_axis=0, tiled=True),
-        lax.all_to_all(filter_pair[1][None], "seq", split_axis=1, concat_axis=0, tiled=True),
+        do_stocks(filter_pair[1][None]),
     )
     input_spectrum = block_forward((moved_data[0], moved_data[1]), block_basis)
     filter_spectrum = block_forward((moved_data[2], moved_data[3]), block_basis)

time: 606 us -> 644 us (1.063)
  local copies, waits for them, and re-layouts: 47.8 us -> 85.3 us
    unnamed x53 -> x116, local copies, waits for them, and re-layouts: 20.7 us -> 58.3 us
  transfers between devices with their start and end apart: 19 -> 19, of which waited for: 13 -> 12; matrix products, arithmetic and copies ran while one was open for 18% -> 17% of each run, Pallas kernels for 0% -> 0%
where the time goes in v1:
time: 644 us; the launch traced here: 634 us
  blocking collectives  252 us (39%)
  starting transfers between devices  123 us (19%)
  local copies, waits for them, and re-layouts  85.3 us (13%)
  waiting for transfers between devices  70.8 us (11%)
  matrix products  70.6 us (11%)
  other arithmetic  17.5 us (3%)
  between operations  14.8 us (2%)
    psum x1, blocking collectives, on_device(): grad_short, grad_skip = lax.psum((short_terms, skip_terms), 'seq')  252 us
    dot_general x36, matrix products, along_rows(): return jnp.tensordot(factor, values, axes=1, precision=exact_mode)  58.4 us
    unnamed x116, local copies, waits for them, and re-layouts  58.3 us
  transfers between devices with their start and end apart: 19, of which 12 were waited for; matrix products, arithmetic and copies ran while one was open for 17% of the time, Pallas kernels for 0%

profile of v1, /device:TPU:128, one launch (start us, length us, event | category | flops | bytes accessed | tf_op | source)
XLA Modules:
  0.0 633.9 jit_solution(16280565844736758536)
XLA Ops:
  47.3 10.5 %all-to-all-start.1 = ((f32[64,1,4,512]{3,2,1,0:T(4,128)}), f32[64,1,4,512]{3,2,1,0:T(4,128)S(1)}, u32[]{:S(2)}, u32[]{:S(2)}) async-start(f32[64,1,4,512]{3,2,1,0:T(4,128)} %constant_dynamic-update-slice_fusion), calls=%async_computation.1 | async-start | bytes 1048576 | tf_op jit(solution)/shard_map/all_to_all | solution.py:82
  63.8 8.9 %all-to-all-done.1 = f32[64,1,4,512]{3,2,1,0:T(4,128)S(1)} async-done(((f32[64,1,4,512]{3,2,1,0:T(4,128)}), f32[64,1,4,512]{3,2,1,0:T(4,128)S(1)}, u32[]{:S(2)}, u32[]{:S(2)}) %all-to-all-start.1) | async-done | bytes 524320 | tf_op jit(solution)/shard_map/all_to_all | solution.py:82
  72.7 8.6 %all-to-all-start = ((f32[1,256,512]{2,0,1:T(1,128)}), f32[1,256,512]{2,0,1:T(1,128)S(1)}, u32[]{:S(2)}, u32[]{:S(2)}) async-start(f32[1,256,512]{2,0,1:T(1,128)} %copy.64), calls=%async_computation | async-start | bytes 1048576 | tf_op jit(solution)/shard_map/all_to_all | solution.py:110
  81.7 6.6 %all-gather.2.cloned.1.call-done = bf16[128,4096]{1,0:T(8,128)(2,1)} async-done(((bf16[128,1024]{1,0:T(8,128)(2,1)}), bf16[128,4096]{1,0:T(8,128)(2,1)}) %all-gather.2.cloned.1.call-update) | async-done | bytes 1048592 | tf_op jit(solution)/shard_map/all_gather | solution.py:129
  88.3 4.8 multiply_reduce_fusion.3
  93.1 3.1 collective-permute-start.2
  102.8 3.1 reduce.7
  106.8 12.0 %all-to-all-start.6 = ((bf16[64,2,1024]{2,1,0:T(2,128)(2,1)}), bf16[64,2,1024]{2,1,0:T(2,128)(2,1)S(1)}, u32[]{:S(2)}, u32[]{:S(2)}) async-start(bf16[64,2,1024]{2,1,0:T(2,128)(2,1)} %reshape.75), calls=%async_computation.7 | async-start | bytes 524288 | tf_op jit(solution)/shard_map/all_to_all | solution.py:150
  128.2 10.3 %all-to-all-start.7 = ((bf16[64,2,1024]{2,1,0:T(2,128)(2,1)}), bf16[64,2,1024]{2,1,0:T(2,128)(2,1)S(1)}, u32[]{:S(2)}, u32[]{:S(2)}) async-start(bf16[64,2,1024]{2,1,0:T(2,128)(2,1)} %reshape.73), calls=%async_computation.8 | async-start | bytes 524288 | tf_op jit(solution)/shard_map/all_to_all | solution.py:153
  144.2 3.5 all-to-all-done.7
  147.8 8.9 %all-to-all-start.3 = ((f32[1,256,512]{2,0,1:T(1,128)}), f32[1,256,512]{2,0,1:T(1,128)S(1)}, u32[]{:S(2)}, u32[]{:S(2)}) async-start(f32[1,256,512]{2,0,1:T(1,128)} %copy.69), calls=%async_computation.3 | async-start | bytes 1048576 | tf_op jit(solution)/shard_map/all_to_all | solution.py:109
  171.4 9.0 %all-to-all-start.2 = ((f32[1,256,512]{2,0,1:T(1,128)}), f32[1,256,512]{2,0,1:T(1,128)S(1)}, u32[]{:S(2)}, u32[]{:S(2)}) async-start(f32[1,256,512]{2,0,1:T(1,128)} %copy.67), calls=%async_computation.2 | async-start | bytes 1048576 | tf_op jit(solution)/shard_map/all_to_all | solution.py:108
  186.8 8.3 %all-to-all-done.2 = f32[1,256,512]{2,0,1:T(1,128)S(1)} async-done(((f32[1,256,512]{2,0,1:T(1,128)}), f32[1,256,512]{2,0,1:T(1,128)S(1)}, u32[]{:S(2)}, u32[]{:S(2)}) %all-to-all-start.2) | async-done | bytes 524320 | tf_op jit(solution)/shard_map/all_to_all | solution.py:108
  200.1 5.8 multiply_subtract_fusion
  209.8 8.7 %all-to-all-start.8 = ((bf16[64,4,512]{2,1,0:T(4,128)(2,1)}), bf16[64,4,512]{2,1,0:T(4,128)(2,1)}, u32[]{:S(2)}, u32[]{:S(2)}) async-start(bf16[64,4,512]{2,1,0:T(4,128)(2,1)} %copy.83), calls=%async_computation.9 | async-start | bytes 524288 | tf_op jit(solution)/shard_map/all_to_all | solution.py:161
  223.8 4.0 all-to-all-done.8
  227.7 9.1 %all-to-all-start.4 = ((f32[64,4,512]{2,1,0:T(4,128)}), f32[64,4,512]{2,1,0:T(4,128)}, u32[]{:S(2)}, u32[]{:S(2)}) async-start(f32[64,4,512]{2,1,0:T(4,128)} %copy.75), calls=%async_computation.4 | async-start | bytes 1048576 | tf_op jit(solution)/shard_map/all_to_all | solution.py:117
  242.1 9.7 %all-to-all-done.4 = f32[64,4,512]{2,1,0:T(4,128)} async-done(((f32[64,4,512]{2,1,0:T(4,128)}), f32[64,4,512]{2,1,0:T(4,128)}, u32[]{:S(2)}, u32[]{:S(2)}) %all-to-all-start.4) | async-done | bytes 524320 | tf_op jit(solution)/shard_map/all_to_all | solution.py:117
  251.7 8.7 %all-to-all-start.5 = ((f32[64,4,512]{2,1,0:T(4,128)}), f32[64,4,512]{2,1,0:T(4,128)}, u32[]{:S(2)}, u32[]{:S(2)}) async-start(f32[64,4,512]{2,1,0:T(4,128)} %copy.76), calls=%async_computation.5 | async-start | bytes 1048576 | tf_op jit(solution)/shard_map/all_to_all | solution.py:118
  268.0 7.2 %all-to-all-done.5 = f32[64,4,512]{2,1,0:T(4,128)} async-done(((f32[64,4,512]{2,1,0:T(4,128)}), f32[64,4,512]{2,1,0:T(4,128)}, u32[]{:S(2)}, u32[]{:S(2)}) %all-to-all-start.5) | async-done | bytes 524320 | tf_op jit(solution)/shard_map/all_to_all | solution.py:118
  275.2 8.7 %all-to-all-start.9 = ((bf16[64,4,512]{2,1,0:T(4,128)(2,1)}), bf16[64,4,512]{2,1,0:T(4,128)(2,1)}, u32[]{:S(2)}, u32[]{:S(2)}) async-start(bf16[64,4,512]{2,1,0:T(4,128)(2,1)} %copy.84), calls=%async_computation.10 | async-start | bytes 524288 | tf_op jit(solution)/shard_map/all_to_all | solution.py:162
  284.2 3.5 fusion.61
  289.7 2.8 fusion.8
  302.3 3.2 collective-permute-done.1
  310.2 5.4 convolution_bitcast_fusion
  315.6 9.1 %copy.89 = f32[4096,512]{1,0:T(8,128)} copy(f32[4096,512]{0,1:T(8,128)} %convolution_bitcast_fusion) | data formatting | bytes 16777216
  327.6 8.5 %all-to-all-start.11 = ((bf16[64,4,512]{2,1,0:T(4,128)(2,1)}), bf16[64,4,512]{2,1,0:T(4,128)(2,1)}, u32[]{:S(2)}, u32[]{:S(2)}) async-start(bf16[64,4,512]{2,1,0:T(4,128)(2,1)} %copy.86), calls=%async_computation.12 | async-start | bytes 524288 | tf_op jit(solution)/shard_map/all_to_all | solution.py:164
  338.7 6.4 %all-to-all-done.11 = bf16[64,4,512]{2,1,0:T(4,128)(2,1)} async-done(((bf16[64,4,512]{2,1,0:T(4,128)(2,1)}), bf16[64,4,512]{2,1,0:T(4,128)(2,1)}, u32[]{:S(2)}, u32[]{:S(2)}) %all-to-all-start.11) | async-done | bytes 262176 | tf_op jit(solution)/shard_map/all_to_all | solution.py:164
  345.1 8.6 %all-to-all-start.10 = ((bf16[64,4,512]{2,1,0:T(4,128)(2,1)}), bf16[64,4,512]{2,1,0:T(4,128)(2,1)S(1)}, u32[]{:S(2)}, u32[]{:S(2)}) async-start(bf16[64,4,512]{2,1,0:T(4,128)(2,1)} %copy.85), calls=%async_computation.11 | async-start | bytes 524288 | tf_op jit(solution)/shard_map/all_to_all | solution.py:163
  354.8 8.2 %all-to-all-done.10 = bf16[64,4,512]{2,1,0:T(4,128)(2,1)S(1)} async-done(((bf16[64,4,512]{2,1,0:T(4,128)(2,1)}), bf16[64,4,512]{2,1,0:T(4,128)(2,1)S(1)}, u32[]{:S(2)}, u32[]{:S(2)}) %all-to-all-start.10) | async-done | bytes 262176 | tf_op jit(solution)/shard_map/all_to_all | solution.py:163
  364.0 4.2 collective-permute-start.3
  372.2 251.6 %all-reduce = (f32[3,3,512]{2,0,1:T(4,128)S(1)}, f32[512]{0:T(512)}) all-reduce(f32[3,3,512]{2,0,1:T(4,128)S(1)} %pad_maximum_fusion.5, f32[512]{0:T(512)S(1)} %get-tuple-element.45), channel_id=1, replica_groups=mesh['seq'=64,'ch'=4] {'seq'}, use_global_device_ids=true, to_apply=%region_4.5 | all-reduce | flops 5120 | bytes 40960 | tf_op jit(solution)/shard_map/psum | solution.py:184
  (211 shorter events, 148.0 us)
Async XLA Ops:
  7.2 74.1 %copy-start.16 = (bf16[128,512]{1,0:T(8,128)(2,1)S(1)}, bf16[128,512]{1,0:T(8,128)(2,1)}, u32[]{:S(2)}) copy-start(bf16[128,512]{1,0:T(8,128)(2,1)} %param.10) | copy-start | bytes 393220
  7.2 74.1 %copy-start.17 = (bf16[128,512]{1,0:T(8,128)(2,1)S(1)}, bf16[128,512]{1,0:T(8,128)(2,1)}, u32[]{:S(2)}) copy-start(bf16[128,512]{1,0:T(8,128)(2,1)} %param.9) | copy-start | bytes 393220
  7.2 74.1 %copy-start.18 = (bf16[128,512]{1,0:T(8,128)(2,1)S(1)}, bf16[128,512]{1,0:T(8,128)(2,1)}, u32[]{:S(2)}) copy-start(bf16[128,512]{1,0:T(8,128)(2,1)} %param.8) | copy-start | bytes 393220
  7.2 56.6 %copy-start.20 = (f32[3,3,512]{2,1,0:T(4,128)S(1)}, f32[3,3,512]{2,1,0:T(4,128)}, u32[]{:S(2)}) copy-start(f32[3,3,512]{2,1,0:T(4,128)} %param.11) | copy-start | bytes 55300
  47.3 25.4 %all-to-all-start.1 = ((f32[64,1,4,512]{3,2,1,0:T(4,128)}), f32[64,1,4,512]{3,2,1,0:T(4,128)S(1)}, u32[]{:S(2)}, u32[]{:S(2)}) async-start(f32[64,1,4,512]{3,2,1,0:T(4,128)} %constant_dynamic-update-slice_fusion), calls=%async_computation.1 | async-start | bytes 1048576 | tf_op jit(solution)/shard_map/all_to_all | solution.py:82
  57.8 30.5 %all-gather.2.cloned.1.call-start = ((), (), s32[]{:S(2)}) async-start(), calls=%async_computation.15 | async-start | bytes 1310720 | tf_op jit(solution)/shard_map/all_gather | solution.py:129
  59.3 22.0 %collective-permute-start = (bf16[3,2,512]{2,1,0:T(2,128)(2,1)S(1)}, bf16[3,2,512]{2,1,0:T(2,128)(2,1)S(1)}, u32[]{:S(2)}, u32[]{:S(2)}) collective-permute-start(bf16[3,2,512]{2,1,0:T(2,128)(2,1)S(1)} %pad_maximum_fusion.6), channel_id=1, source_target_pairs={{0,4},{4,8},{8,12},{12,16},{16,20},{20,24},{24,28},{28,32},{32,36}... | collective-permute-start | bytes 18440 | tf_op jit(solution)/shard_map/ppermute | solution.py:14
  72.7 34.1 %all-to-all-start = ((f32[1,256,512]{2,0,1:T(1,128)}), f32[1,256,512]{2,0,1:T(1,128)S(1)}, u32[]{:S(2)}, u32[]{:S(2)}) async-start(f32[1,256,512]{2,0,1:T(1,128)} %copy.64), calls=%async_computation | async-start | bytes 1048576 | tf_op jit(solution)/shard_map/all_to_all | solution.py:110
  81.7 19.3 %copy-start.6 = (f32[3,128,512]{2,1,0:T(8,128)}, f32[3,128,512]{2,1,0:T(8,128)S(1)}, u32[]{:S(2)}) copy-start(f32[3,128,512]{2,1,0:T(8,128)S(1)} %multiply_add_fusion.3) | copy-start | bytes 2359300
  93.1 5.6 collective-permute-start.2
  106.8 21.4 %all-to-all-start.6 = ((bf16[64,2,1024]{2,1,0:T(2,128)(2,1)}), bf16[64,2,1024]{2,1,0:T(2,128)(2,1)S(1)}, u32[]{:S(2)}, u32[]{:S(2)}) async-start(bf16[64,2,1024]{2,1,0:T(2,128)(2,1)} %reshape.75), calls=%async_computation.7 | async-start | bytes 524288 | tf_op jit(solution)/shard_map/all_to_all | solution.py:150
  128.2 29.7 %copy-start.13 = (bf16[64,2,1024]{2,1,0:T(2,128)(2,1)}, bf16[64,2,1024]{2,1,0:T(2,128)(2,1)S(1)}, u32[]{:S(2)}) copy-start(bf16[64,2,1024]{2,1,0:T(2,128)(2,1)S(1)} %all-to-all-done.6) | copy-start | bytes 786436
  128.2 19.5 %all-to-all-start.7 = ((bf16[64,2,1024]{2,1,0:T(2,128)(2,1)}), bf16[64,2,1024]{2,1,0:T(2,128)(2,1)S(1)}, u32[]{:S(2)}, u32[]{:S(2)}) async-start(bf16[64,2,1024]{2,1,0:T(2,128)(2,1)} %reshape.73), calls=%async_computation.8 | async-start | bytes 524288 | tf_op jit(solution)/shard_map/all_to_all | solution.py:153
  147.8 10.1 %copy-start.14 = (bf16[64,2,1024]{2,1,0:T(2,128)(2,1)}, bf16[64,2,1024]{2,1,0:T(2,128)(2,1)S(1)}, u32[]{:S(2)}) copy-start(bf16[64,2,1024]{2,1,0:T(2,128)(2,1)S(1)} %all-to-all-done.7) | copy-start | bytes 786436
  147.8 23.7 %all-to-all-start.3 = ((f32[1,256,512]{2,0,1:T(1,128)}), f32[1,256,512]{2,0,1:T(1,128)S(1)}, u32[]{:S(2)}, u32[]{:S(2)}) async-start(f32[1,256,512]{2,0,1:T(1,128)} %copy.69), calls=%async_computation.3 | async-start | bytes 1048576 | tf_op jit(solution)/shard_map/all_to_all | solution.py:109
  171.4 23.7 %all-to-all-start.2 = ((f32[1,256,512]{2,0,1:T(1,128)}), f32[1,256,512]{2,0,1:T(1,128)S(1)}, u32[]{:S(2)}, u32[]{:S(2)}) async-start(f32[1,256,512]{2,0,1:T(1,128)} %copy.67), calls=%async_computation.2 | async-start | bytes 1048576 | tf_op jit(solution)/shard_map/all_to_all | solution.py:108
  209.8 17.9 %all-to-all-start.8 = ((bf16[64,4,512]{2,1,0:T(4,128)(2,1)}), bf16[64,4,512]{2,1,0:T(4,128)(2,1)}, u32[]{:S(2)}, u32[]{:S(2)}) async-start(bf16[64,4,512]{2,1,0:T(4,128)(2,1)} %copy.83), calls=%async_computation.9 | async-start | bytes 524288 | tf_op jit(solution)/shard_map/all_to_all | solution.py:161
  227.7 24.0 %all-to-all-start.4 = ((f32[64,4,512]{2,1,0:T(4,128)}), f32[64,4,512]{2,1,0:T(4,128)}, u32[]{:S(2)}, u32[]{:S(2)}) async-start(f32[64,4,512]{2,1,0:T(4,128)} %copy.75), calls=%async_computation.4 | async-start | bytes 1048576 | tf_op jit(solution)/shard_map/all_to_all | solution.py:117
  251.7 23.5 %all-to-all-start.5 = ((f32[64,4,512]{2,1,0:T(4,128)}), f32[64,4,512]{2,1,0:T(4,128)}, u32[]{:S(2)}, u32[]{:S(2)}) async-start(f32[64,4,512]{2,1,0:T(4,128)} %copy.76), calls=%async_computation.5 | async-start | bytes 1048576 | tf_op jit(solution)/shard_map/all_to_all | solution.py:118
  263.3 37.0 %copy-start.21 = (f32[512]{0:T(512)S(1)}, f32[512]{0:T(512)}, u32[]{:S(2)}) copy-start(f32[512]{0:T(512)} %param.13) | copy-start | bytes 6148
  265.9 39.5 %copy-start.15 = (f32[128,512]{1,0:T(8,128)S(1)}, f32[128,512]{1,0:T(8,128)}, u32[]{:S(2)}) copy-start(f32[128,512]{1,0:T(8,128)} %get-tuple-element.70) | copy-start | bytes 786436
  275.2 23.4 %all-to-all-start.9 = ((bf16[64,4,512]{2,1,0:T(4,128)(2,1)}), bf16[64,4,512]{2,1,0:T(4,128)(2,1)}, u32[]{:S(2)}, u32[]{:S(2)}) async-start(bf16[64,4,512]{2,1,0:T(4,128)(2,1)} %copy.84), calls=%async_computation.10 | async-start | bytes 524288 | tf_op jit(solution)/shard_map/all_to_all | solution.py:162
  284.0 23.3 %copy-start.7 = (f32[3,128,512]{2,1,0:T(8,128)S(1)}, f32[3,128,512]{2,1,0:T(8,128)}, u32[]{:S(2)}) copy-start(f32[3,128,512]{2,1,0:T(8,128)} %copy-done.6) | copy-start | bytes 2359300
  284.0 341.4 %reduce-scatter.5.cloned.1.call-start = ((), (), s32[]{:S(2)}) async-start(), calls=%async_computation.14 | async-start | bytes 2621440 | tf_op jit(solution)/shard_map/reduce_scatter | solution.py:126
  294.1 11.3 %collective-permute-start.1 = (f32[128,512]{1,0:T(8,128)}, f32[128,512]{1,0:T(8,128)}, u32[]{:S(2)}, u32[]{:S(2)}) collective-permute-start(f32[128,512]{1,0:T(8,128)} %slice.82), channel_id=1, source_target_pairs={{0,4},{4,8},{8,12},{12,16},{16,20},{20,24},{24,28},{28,32},{32,36}... | collective-permute-start | bytes 786440 | tf_op jit(solution)/shard_map/ppermute | solution.py:14
  307.4 56.4 %copy-start.9 = (f32[1,128,512]{2,1,0:T(8,128)}, f32[1,128,512]{2,1,0:T(8,128)S(1)}, u32[]{:S(2)}) copy-start(f32[1,128,512]{2,1,0:T(8,128)S(1)} %get-tuple-element.61) | copy-start | bytes 786436
  310.1 317.0 %reduce-scatter.7.cloned.1.call-start = ((), (), s32[]{:S(2)}) async-start(), calls=%async_computation.16 | async-start | bytes 8519680
  327.6 17.5 %all-to-all-start.11 = ((bf16[64,4,512]{2,1,0:T(4,128)(2,1)}), bf16[64,4,512]{2,1,0:T(4,128)(2,1)}, u32[]{:S(2)}, u32[]{:S(2)}) async-start(bf16[64,4,512]{2,1,0:T(4,128)(2,1)} %copy.86), calls=%async_computation.12 | async-start | bytes 524288 | tf_op jit(solution)/shard_map/all_to_all | solution.py:164
  337.0 26.9 %copy-start.10 = (f32[1,128,512]{2,1,0:T(8,128)S(1)}, f32[1,128,512]{2,1,0:T(8,128)}, u32[]{:S(2)}) copy-start(f32[1,128,512]{2,1,0:T(8,128)} %get-tuple-element.48) | copy-start | bytes 786436
  345.1 17.9 %all-to-all-start.10 = ((bf16[64,4,512]{2,1,0:T(4,128)(2,1)}), bf16[64,4,512]{2,1,0:T(4,128)(2,1)S(1)}, u32[]{:S(2)}, u32[]{:S(2)}) async-start(bf16[64,4,512]{2,1,0:T(4,128)(2,1)} %copy.85), calls=%async_computation.11 | async-start | bytes 524288 | tf_op jit(solution)/shard_map/all_to_all | solution.py:163
  364.0 5.7 collective-permute-start.3
  369.6 257.5 %copy-start.1 = (f32[128,512]{1,0:T(8,128)S(1)}, f32[128,512]{1,0:T(8,128)}, u32[]{:S(2)}) copy-start(f32[128,512]{1,0:T(8,128)} %param.12) | copy-start | bytes 786436
  (9 other events, 17.6 us)
Sparse Core Ops, SparseCore 0:
  60.5 27.7 all-gather.1
  310.3 30.2 reduce-scatter.4
  345.9 149.4 reduce-scatter.6
